TPU v7x, 32 devices: a whole 2x2x4 slice. The times are simulated.
32 devices in a mesh: groups: 2 (over x), ctx: 16 (over z, y, core).
Axes of the slice: x: 2, y: 2, z: 4, core: 2. Of those that a mesh axis runs over, the one named last changes fastest.
Arguments:
- queries: bfloat16 [4096, 2048], P(('groups', 'ctx')), parts along dimension 0, may hold values from -64 to 64
- keys: bfloat16 [4096, 512], P(('groups', 'ctx')), parts along dimension 0, may hold values from -6 to 6
- values: bfloat16 [4096, 512], P(('groups', 'ctx')), parts along dimension 0, may hold values from -6 to 6
- block_ids: int32 [4096], P(('groups', 'ctx')), parts along dimension 0, may hold values from 0 to 3, as said below
- out_weight: bfloat16 [2048, 2048], P('ctx'), may hold values from -0.59765625 to 0.59765625
- summary_gain: float32 [128], replicated, may hold values from 0.1 to 1.9
- norm_gain: float32 [2048], replicated, may hold values from 0.1 to 1.9
- routes: int32 [4096, 8], P(('groups', 'ctx')), parts along dimension 0, may hold values from 0 to 15, all different within a row; in each aligned block of 128 rows (0 to 127, 128 to 255, ...) at most 80 rows name the same one
- route_scores: float32 [4096, 8], P(('groups', 'ctx')), parts along dimension 0, may hold values from 0.02 to 1
- expert_gate: bfloat16 [16, 2048, 768], P('ctx'), may hold values from -0.125 to 0.125
- expert_up: bfloat16 [16, 2048, 768], P('ctx'), may hold values from -0.125 to 0.125
- expert_down: bfloat16 [16, 768, 2048], P('ctx'), may hold values from -0.21875 to 0.21875
Outputs:
- projected: bfloat16 [4096, 2048], P(('groups', 'ctx')), parts along dimension 0
- mixed: bfloat16 [4096, 2048], P(('groups', 'ctx')), parts along dimension 0
There are 2 independent parts, one for each index of `groups`. A program takes and returns all parts, laid end to end along the dimension named above; an argument that names none is the same for every part. Nothing has to cross between parts.
Inputs may be any that keep to these rules, and one draw needn't show every extreme that they name: `block_ids`: within each context shard's 128 tokens the block numbers never fall, start at 0 and take every value up to 3. `routes`: among the 128 tokens of one context shard no expert is chosen more than 80 times, and in every draw some expert is chosen exactly 80 times by some shard. A token's 8 experts differ.
All inputs are finite; a program needn't handle non-finite values.
Results may differ from a plain program's by a relative error of at most 0.0077.
Values may be sent and summed in bfloat16 or wider, within the bound.
A program may use at most 128 MiB of HBM per device.

v0:
```python
import functools
import math

import jax
import jax.numpy as jnp
from jax import lax
from jax.experimental import pallas as pl
from jax.experimental.pallas import tpu as pltpu
from jax.sharding import PartitionSpec as P

D = 2048
HQ = 16
KVH = 4
HD = 128
TOP = 8
EXP_DEV = 1
NB = 4


def normalize(x):
    return x * lax.rsqrt(jnp.mean(x * x, axis=-1, keepdims=True) + 1e-06)


RING_BYTES = 16 * 2**20


def chip_at(position, chips):
    depth = chips // 2
    y = position // depth
    return (position * (1 - y) + (chips - 1 - position) * y) * 2 + y


def layer_kernel(
    n,
    cap,
    queries,
    keys,
    values,
    blocks,
    weight_own,
    key_gain,
    norm_gain,
    routes,
    route_scores,
    gate_hbm,
    up_hbm,
    down_hbm,
    projected,
    out,
    normed,
    hidden,
    att,
    wg,
    sums_own,
    sums,
    share,
    gate_w,
    up_w,
    down_w,
    tok,
    wbuf,
    rows_in,
    act,
    place,
    comb,
    mine,
    outgo,
    theirs,
    ring_in,
    load_sem,
    s_send,
    s_recv,
    wg_send,
    wg_recv,
    wx_send,
    wx_recv,
    wp_send,
    wp_recv,
    w_send,
    w_recv,
    ag_send,
    ag_recv,
    pt_send,
    pt_recv,
    y_send,
    y_recv,
    rs_send_sem,
    rs_recv_sem,
):
    tokens = normed.shape[0]
    half = tokens // 2
    width = normed.shape[1]
    ff = gate_w.shape[1]
    chips = n // 2
    far = chips // 2
    me = lax.axis_index("ctx")
    core = me % 2
    y = (me // 2) % 2
    z = me // 4
    pos = z * (1 - y) + (chips - 1 - z) * y
    partner = me + 1 - 2 * core
    ahead = chip_at((pos + 1) % chips, chips) * 2 + core
    behind = chip_at((pos + chips - 1) % chips, chips) * 2 + core
    neighbour = (ahead, behind)

    loads = [
        pltpu.make_async_copy(a, b, load_sem.at[k])
        for k, (a, b) in enumerate(((gate_hbm, gate_w), (up_hbm, up_w), (down_hbm, down_w)))
    ]
    for load in loads:
        load.start()

    barrier = pltpu.get_barrier_semaphore()
    across = 1 - lax.axis_index("groups")

    def greet(k, _):
        pl.semaphore_signal(barrier, inc=1, device_id={"ctx": (me + k) % n})
        return 0

    lax.fori_loop(1, n, greet, 0)
    pl.semaphore_signal(barrier, inc=1, device_id={"groups": across})

    def mean_of(ref):
        shape = (2 * NB, tokens)
        ids = jnp.broadcast_to(blocks[...], shape)
        member = jnp.where(ids == lax.broadcasted_iota(jnp.int32, shape, 0) % NB, 1.0, 0.0)
        count = jnp.sum(member, axis=1, keepdims=True)
        return (
            jnp.dot(member.astype(jnp.bfloat16), ref[...], preferred_element_type=jnp.float32)
            / count
        )

    kmean, vmean = mean_of(keys), mean_of(values)
    upper = lax.broadcasted_iota(jnp.int32, (2 * NB, HD), 0) < NB
    for g in range(KVH):
        cols = slice(g * HD, (g + 1) * HD)
        sums_own[:, cols] = jnp.where(
            upper, normalize(kmean[:, cols]) * key_gain[...], normalize(vmean[:, cols])
        ).astype(jnp.bfloat16)
    pl.semaphore_wait(barrier, n)

    def s_copy(k):
        target = (me + k) % n
        return pltpu.make_async_remote_copy(
            src_ref=sums_own,
            dst_ref=sums.at[me],
            send_sem=s_send.at[k],
            recv_sem=s_recv.at[k],
            device_id={"ctx": target},
        )

    def s_start(k, _):
        s_copy(k).start()
        return 0

    def s_wait(k, _):
        s_copy(k).wait()
        return 0

    lax.fori_loop(1, n, s_start, 0)
    sums[me] = sums_own[...]

    def rows(h):
        return pl.ds(h * half, half)

    def chip(offset):
        return (pos + offset + chips) % chips

    def ag_copy(d, step, h):
        sign = 1 - 2 * d
        q = chip(-sign * (step - 1))
        src = normed.at[rows(h)] if step == 1 else tok.at[q, core, rows(h)]
        return pltpu.make_async_remote_copy(
            src_ref=src,
            dst_ref=tok.at[q, core, rows(h)],
            send_sem=ag_send.at[d, step - 1, h],
            recv_sem=ag_recv.at[d, step - 1, h],
            device_id={"ctx": neighbour[d]},
        )

    def pt_copy(offset, h):
        q = chip(offset)
        src = normed.at[rows(h)] if offset == 0 else tok.at[q, core, rows(h)]
        return pltpu.make_async_remote_copy(
            src_ref=src,
            dst_ref=tok.at[q, core, rows(h)],
            send_sem=pt_send.at[offset % chips, h],
            recv_sem=pt_recv.at[offset % chips, h],
            device_id={"ctx": partner},
        )

    def order(d):
        return (0, 1) if d == 0 else (1, 0)

    wrows = weight_own.shape[0]
    side = wrows // 4
    middle = wrows - 2 * side
    group = 1 - across
    mine_side = group * (side + middle)
    other_side = across * (side + middle)

    def w_rows(kind):
        if kind == 0:
            return mine_side, side
        if kind == 1:
            return side, middle
        return other_side, side

    def w_at(q, kind):
        start, size = w_rows(kind)
        return wg.at[q, pl.ds(core * wrows + start, size)]

    def w_first(kind):
        start, size = w_rows(kind)
        return weight_own.at[pl.ds(start, size)]

    def wg_copy(d, step, h):
        sign = 1 - 2 * d
        q = chip(-sign * (step - 1))
        return pltpu.make_async_remote_copy(
            src_ref=w_first(h) if step == 1 else w_at(q, h),
            dst_ref=w_at(q, h),
            send_sem=wg_send.at[d, step - 1, h],
            recv_sem=wg_recv.at[d, step - 1, h],
            device_id={"ctx": neighbour[d]},
        )

    def wx_copy(offset):
        q = chip(offset)
        return pltpu.make_async_remote_copy(
            src_ref=w_at(q, 0),
            dst_ref=w_at(q, 0),
            send_sem=wx_send.at[offset % chips],
            recv_sem=wx_recv.at[offset % chips],
            device_id={"groups": across},
        )

    def wp_copy(offset, kind):
        q = chip(offset)
        return pltpu.make_async_remote_copy(
            src_ref=w_first(kind) if offset == 0 else w_at(q, kind),
            dst_ref=w_at(q, kind),
            send_sem=wp_send.at[offset % chips, kind],
            recv_sem=wp_recv.at[offset % chips, kind],
            device_id={"ctx": partner},
        )

    for k in range(2):
        for d in range(2):
            wg_copy(d, 1, order(d)[k]).start()
    for kind in range(3):
        wp_copy(0, kind).start()
    wg[pos, pl.ds(pl.multiple_of(core * wrows, wrows), wrows)] = weight_own[...]

    def w_copy(k):
        target = (me + k) % n
        return pltpu.make_async_remote_copy(
            src_ref=share.at[target],
            dst_ref=wbuf.at[pos * 2 + core],
            send_sem=w_send.at[k],
            recv_sem=w_recv.at[k],
            device_id={"ctx": target},
        )

    def w_start(k, _):
        w_copy(k).start()
        return 0

    def w_wait(k, _):
        w_copy(k).wait()
        return 0

    chosen_scores = route_scores[...]
    combine = chosen_scores / jnp.sum(chosen_scores, axis=0, keepdims=True)
    expert = lax.broadcasted_iota(jnp.int32, (n, tokens), 0)
    table_of = jnp.zeros((n, tokens), jnp.float32)
    for c in range(TOP):
        table_of = table_of + jnp.where(routes[c : c + 1] == expert, combine[c : c + 1], 0.0)
    for e in range(n):
        share[e] = jnp.broadcast_to(table_of[e : e + 1], (8, tokens))
    lax.fori_loop(1, n, w_start, 0)
    wbuf[pos * 2 + core] = share[me]
    lax.fori_loop(1, n, s_wait, 0)

    many = HQ // KVH
    scale = 1.0 / math.sqrt(HD)
    tall = (many * tokens, tokens)
    causal = lax.broadcasted_iota(jnp.int32, tall, 0) % tokens >= lax.broadcasted_iota(
        jnp.int32, tall, 1
    )
    far_shape = (many * tokens, n * 2 * NB)
    entry = lax.broadcasted_iota(jnp.int32, far_shape, 1)
    seen = (entry % (2 * NB) < NB) & (entry // (2 * NB) < me)
    contract_last = (((1,), (1,)), ((), ()))

    def attend(g):
        cols = slice(g * HD, (g + 1) * HD)
        heads = [slice((g * many + i) * HD, (g * many + i + 1) * HD) for i in range(many)]
        q = jnp.concatenate([queries[:, c] for c in heads], axis=0)
        table = sums[:, :, cols].astype(jnp.float32).reshape(n * 2 * NB, HD)
        shifted = jnp.concatenate([table[NB:], table[:NB]], axis=0).astype(jnp.bfloat16)
        table = table.astype(jnp.bfloat16)
        near = (
            lax.dot_general(q, keys[:, cols], contract_last, preferred_element_type=jnp.float32)
            * scale
        )
        near = jnp.where(causal, near, -jnp.inf)
        remote = lax.dot_general(q, table, contract_last, preferred_element_type=jnp.float32) * scale
        remote = jnp.where(seen, remote, -jnp.inf)
        top = jnp.maximum(
            jnp.max(near, axis=1, keepdims=True), jnp.max(remote, axis=1, keepdims=True)
        )
        near, remote = jnp.exp(near - top), jnp.exp(remote - top)
        total = jnp.sum(near, axis=1, keepdims=True) + jnp.sum(remote, axis=1, keepdims=True)
        near, remote = (near / total).astype(jnp.bfloat16), (remote / total).astype(jnp.bfloat16)
        result = jnp.dot(
            near, values[:, cols], preferred_element_type=jnp.float32
        ) + jnp.dot(remote, shifted, preferred_element_type=jnp.float32)
        result = result.astype(jnp.bfloat16)
        for i, c in enumerate(heads):
            att[:, c] = result[i * tokens : (i + 1) * tokens]

    def project(offset):
        q = chip(offset)
        for kind in range(3):
            wp_copy(offset, kind).wait_recv()
        place_at = pl.multiple_of(chip_at(q, chips) * 2 * wrows, 2 * wrows)
        left = att[:, pl.ds(place_at, 2 * wrows)]

        def tile(k, _):
            cols = pl.ds(pl.multiple_of(k * 512, 512), 512)
            part = jnp.dot(left, wg[q, :, cols], preferred_element_type=jnp.float32)
            hidden[:, cols] = part if offset == 0 else hidden[:, cols] + part
            return 0

        lax.fori_loop(0, width // 512, tile, 0)

    def w_step(step, k):
        for d in range(2):
            h = order(d)[k]
            sign = 1 - 2 * d
            wg_copy(d, step, h).wait_recv()
            if step + 1 < far or (step + 1 == far and k == 0):
                wg_copy(d, step + 1, h).start()
            if h == 0:
                wx_copy(-sign * step).start()
            wp_copy(-sign * step, h).start()

    def x_step(offset):
        wx_copy(offset).wait_recv()
        wp_copy(offset, 2).start()

    attend(0)
    attend(1)
    w_step(1, 0)
    attend(2)
    w_step(1, 1)
    attend(3)
    for step in range(2, far):
        w_step(step, 0)
        x_step(1 - step)
        x_step(step - 1)
        if step == 2:
            project(0)
        else:
            project(2 - step)
        w_step(step, 1)
        if step > 2:
            project(step - 2)
    w_step(far, 0)
    x_step(1 - far)
    x_step(far - 1)
    project(2 - far)
    project(far - 2)
    x_step(far)
    project(1 - far)
    project(far - 1)
    project(far)
    for h in range(2):
        hid = hidden[rows(h)]
        projected[rows(h)] = hid.astype(jnp.bfloat16)
        tidy = (normalize(hid) * norm_gain[...]).astype(jnp.bfloat16)
        normed[rows(h)] = tidy
        tok[pos, core, rows(h)] = tidy

    for k in range(2):
        for d in range(2):
            ag_copy(d, 1, order(d)[k]).start()
    for h in range(2):
        pt_copy(0, h).start()

    lax.fori_loop(1, n, w_wait, 0)
    for load in loads:
        load.wait()

    def y_copy(offset):
        q = chip(offset)
        return pltpu.make_async_remote_copy(
            src_ref=outgo.at[q],
            dst_ref=theirs.at[q],
            send_sem=y_send.at[offset % chips],
            recv_sem=y_recv.at[offset % chips],
            device_id={"ctx": partner},
        )

    def compute(offset):
        q = chip(offset)
        for h in range(2):
            pt_copy(offset, h).wait_recv()
        earlier = lax.broadcasted_iota(jnp.int32, (tokens, tokens), 0) < lax.broadcasted_iota(
            jnp.int32, (tokens, tokens), 1
        )
        earlier = jnp.where(earlier, 1.0, 0.0).astype(jnp.bfloat16)
        line = lax.broadcasted_iota(jnp.int32, (cap, tokens), 0).astype(jnp.float32)
        for rel in range(2):
            side = (core + rel) % 2
            weight = wbuf[q * 2 + side]
            chosen = jnp.where(weight > 0.0, 1.0, 0.0)
            slot = jnp.dot(chosen.astype(jnp.bfloat16), earlier, preferred_element_type=jnp.float32)
            slot = jnp.where(weight > 0.0, slot, -1.0)
            hit = jnp.broadcast_to(slot[0:1], (cap, tokens)) == line
            pick = jnp.where(hit, 1.0, 0.0).astype(jnp.bfloat16)
            place[rel] = pick
            scaled = jnp.where(hit, jnp.broadcast_to(weight[0:1], (cap, tokens)), 0.0)
            comb[rel] = jnp.broadcast_to(jnp.sum(scaled, axis=1, keepdims=True), (cap, 128))
            for c in range(0, width, 512):
                rows_in[rel * cap : (rel + 1) * cap, c : c + 512] = jnp.dot(
                    pick, tok[q, side, :, c : c + 512], preferred_element_type=jnp.float32
                ).astype(jnp.bfloat16)

        def in_tile(k, _):
            cols = pl.ds(pl.multiple_of(k * 256, 256), 256)
            x = rows_in[...]
            g = jnp.dot(x, gate_w[:, cols], preferred_element_type=jnp.float32)
            u = jnp.dot(x, up_w[:, cols], preferred_element_type=jnp.float32)
            act[:, cols] = (g / (1.0 + jnp.exp(-g)) * u).astype(jnp.bfloat16)
            return 0

        lax.fori_loop(0, ff // 256, in_tile, 0)

        def out_tile(k, _):
            cols = pl.ds(pl.multiple_of(k * 512, 512), 512)
            r = jnp.dot(act[...], down_w[:, cols], preferred_element_type=jnp.float32)
            r = r.astype(jnp.bfloat16).astype(jnp.float32)
            for rel, dest in ((0, mine), (1, outgo)):
                part = r[rel * cap : (rel + 1) * cap] * comb[rel][:, 0:1]
                dest[q, :, cols] = lax.dot_general(
                    place[rel],
                    part.astype(jnp.bfloat16),
                    (((0,), (0,)), ((), ())),
                    preferred_element_type=jnp.float32,
                ).astype(jnp.bfloat16)
            return 0

        lax.fori_loop(0, width // 512, out_tile, 0)
        y_copy(offset).start()

    for step in range(1, far):
        for k in range(2):
            for d in range(2):
                h = order(d)[k]
                sign = 1 - 2 * d
                ag_copy(d, step, h).wait_recv()
                if step + 1 < far or k == 0:
                    ag_copy(d, step + 1, h).start()
                pt_copy(-sign * step, h).start()
            if step == 1:
                if k == 0:
                    compute(0)
            else:
                compute((step - 1) * (2 * k - 1))
    compute(1 - far)
    compute(far - 1)
    for d in range(2):
        h = order(d)[0]
        ag_copy(d, far, h).wait_recv()
        pt_copy(far, h).start()

    def sum_of(q, h):
        return mine[q, rows(h)].astype(jnp.float32) + theirs[q, rows(h)].astype(jnp.float32)

    def rs_copy(d, step, h, src):
        return pltpu.make_async_remote_copy(
            src_ref=src,
            dst_ref=ring_in.at[d, step - 1, h],
            send_sem=rs_send_sem.at[d, step - 1, h],
            recv_sem=rs_recv_sem.at[d, step - 1, h],
            device_id={"ctx": neighbour[d]},
        )

    def rs_step(d, step, k):
        h = order(d)[k]
        sign = 1 - 2 * d
        q = chip(sign * (far + 1 - step))
        if step == 1 or (step == 2 and k == 1):
            mine[q, rows(h)] = sum_of(q, h).astype(jnp.bfloat16)
            src = mine.at[q, rows(h)]
        else:
            src = ring_in.at[d, step - 2, h]
            rs_copy(d, step - 1, h, src).wait_recv()
            ring_in[d, step - 2, h] = (
                ring_in[d, step - 2, h].astype(jnp.float32) + sum_of(q, h)
            ).astype(jnp.bfloat16)
        rs_copy(d, step, h, src).start()

    for offset in range(chips):
        if offset != far:
            y_copy(offset).wait_recv()
    for d in range(2):
        rs_step(d, 2, 1)
    compute(far)
    y_copy(far).wait_recv()
    sends = [(1, 0)]
    for step in range(2, far + 1):
        if step < far:
            sends += [(step + 1, 1)]
        sends += [(step, 0)]
    for step, k in sends:
        for d in range(2):
            rs_step(d, step, k)
    for h in range(2):
        total = hidden[rows(h)] + sum_of(pos, h)
        for d in range(2):
            rs_copy(d, far, h, ring_in.at[d, far - 1, h]).wait_recv()
            total = total + ring_in[d, far - 1, h].astype(jnp.float32)
        out[rows(h)] = total.astype(jnp.bfloat16)

    for d in range(2):
        for step in range(1, far + 1):
            for k in range(2):
                h = order(d)[k]
                if step < far or k == 0:
                    ag_copy(d, step, h).wait_send()
                if step > 1 or k == 0:
                    rs_copy(d, step, h, ring_in.at[d, step - 1, h]).wait_send()
    for offset in range(chips):
        for h in range(2):
            pt_copy(offset, h).wait_send()
        y_copy(offset).wait_send()


    for d in range(2):
        for step in range(1, far + 1):
            for k in range(2):
                if step < far or k == 0:
                    wg_copy(d, step, order(d)[k]).wait_send()
    for offset in range(chips):
        if offset > 0:
            wx_copy(offset).wait_send()
        for kind in range(3):
            wp_copy(offset, kind).wait_send()


def write_kernel(a, b, a_out, b_out, sem):
    copies = [
        pltpu.make_async_copy(x, y, sem.at[k]) for k, (x, y) in enumerate(((a, a_out), (b, b_out)))
    ]
    for copy in copies:
        copy.start()
    for copy in copies:
        copy.wait()


def layer_ring(
    queries,
    keys,
    values,
    block_ids,
    out_weight,
    summary_gain,
    norm_gain,
    routes,
    route_scores,
    expert_gate,
    expert_up,
    expert_down,
    n,
    cap,
):
    tokens, width = queries.shape
    ff = expert_gate.shape[-1]
    chips = n // 2
    far = chips // 2
    vmem = pl.BlockSpec(memory_space=pltpu.VMEM)
    hbm = pl.BlockSpec(memory_space=pl.ANY)
    dma = pltpu.SemaphoreType.DMA
    bf16, f32 = jnp.bfloat16, jnp.float32
    result = jax.ShapeDtypeStruct((tokens, width), bf16)
    pair = pl.pallas_call(
        functools.partial(layer_kernel, n, cap),
        out_shape=(result, result),
        in_specs=[vmem] * 9 + [hbm] * 3,
        out_specs=(vmem, vmem),
        scratch_shapes=[
            pltpu.VMEM((tokens, width), bf16),
            pltpu.VMEM((tokens, width), f32),
            pltpu.VMEM((tokens, width), bf16),
            pltpu.VMEM((chips, 2 * out_weight.shape[0], width), bf16),
            pltpu.VMEM((2 * NB, KVH * HD), bf16),
            pltpu.VMEM((n, 2 * NB, KVH * HD), bf16),
            pltpu.VMEM((n, 8, tokens), f32),
            pltpu.VMEM((width, ff), bf16),
            pltpu.VMEM((width, ff), bf16),
            pltpu.VMEM((ff, width), bf16),
            pltpu.VMEM((chips, 2, tokens, width), bf16),
            pltpu.VMEM((n, 8, tokens), f32),
            pltpu.VMEM((2 * cap, width), bf16),
            pltpu.VMEM((2 * cap, ff), bf16),
            pltpu.VMEM((2, cap, tokens), bf16),
            pltpu.VMEM((2, cap, 128), f32),
            pltpu.VMEM((chips, tokens, width), bf16),
            pltpu.VMEM((chips, tokens, width), bf16),
            pltpu.VMEM((chips, tokens, width), bf16),
            pltpu.VMEM((2, far, 2, tokens // 2, width), bf16),
            dma((3,)),
            dma((n,)),
            dma((n,)),
            dma((2, far, 2)),
            dma((2, far, 2)),
            dma((chips,)),
            dma((chips,)),
            dma((chips, 3)),
            dma((chips, 3)),
            dma((n,)),
            dma((n,)),
            dma((2, far, 2)),
            dma((2, far, 2)),
            dma((chips, 2)),
            dma((chips, 2)),
            dma((chips,)),
            dma((chips,)),
            dma((2, far, 2)),
            dma((2, far, 2)),
        ],
        compiler_params=pltpu.CompilerParams(
            collective_id=1, has_side_effects=True, vmem_limit_bytes=62 * 2**20
        ),
    )(
        queries,
        keys,
        values,
        block_ids[None, :],
        out_weight,
        summary_gain[None, :],
        norm_gain[None, :],
        routes.T,
        route_scores.T,
        expert_gate[0],
        expert_up[0],
        expert_down[0],
    )
    return pl.pallas_call(
        write_kernel,
        out_shape=(result, result),
        in_specs=[vmem] * 2,
        out_specs=(hbm, hbm),
        scratch_shapes=[dma((2,))],
    )(*pair)


def body(
    queries,
    keys,
    values,
    block_ids,
    out_weight,
    summary_gain,
    norm_gain,
    routes,
    route_scores,
    expert_gate,
    expert_up,
    expert_down,
):
    tokens_here = queries.shape[0]
    combine = route_scores / jnp.sum(route_scores, axis=-1, keepdims=True)
    experts_all = EXP_DEV * lax.axis_size("ctx")
    capacity = max(2, 5 * tokens_here * TOP // (4 * experts_all))
    chips = experts_all // 2
    fits = experts_all * tokens_here * D * 2 <= RING_BYTES
    if fits and chips % 4 == 0 and lax.axis_size("groups") == 2:
        return layer_ring(
            queries,
            keys,
            values,
            block_ids,
            out_weight,
            summary_gain,
            norm_gain,
            routes,
            route_scores,
            expert_gate,
            expert_up,
            expert_down,
            experts_all,
            -(-capacity // 16) * 16,
        )
    group = HQ // KVH
    scale = 1.0 / math.sqrt(HD)
    member = block_ids[None, :] == jnp.arange(NB, dtype=jnp.int32)[:, None]
    count = jnp.sum(member.astype(jnp.float32), axis=-1)
    indicator = member.astype(jnp.bfloat16)
    kmean = jnp.dot(indicator, keys, preferred_element_type=jnp.float32) / count[:, None]
    vmean = jnp.dot(indicator, values, preferred_element_type=jnp.float32) / count[:, None]
    summary_keys = (
        (normalize(kmean.reshape(NB, KVH, HD)) * summary_gain)
        .astype(jnp.bfloat16)
        .reshape(NB, KVH * HD)
    )
    summary_values = (
        normalize(vmean.reshape(NB, KVH, HD)).astype(jnp.bfloat16).reshape(NB, KVH * HD)
    )
    summaries = lax.all_gather(
        jnp.concatenate([summary_keys, summary_values], axis=1), "ctx", axis=0, tiled=True
    )
    all_keys, all_values = summaries[:, : KVH * HD], summaries[:, KVH * HD :]
    index = lax.axis_index("ctx")
    query = queries.reshape(tokens_here, KVH, group, HD)
    key_loc = keys.reshape(tokens_here, KVH, HD)
    remote_keys = all_keys.reshape(-1, KVH, HD)
    causal = jnp.arange(tokens_here)[:, None] >= jnp.arange(tokens_here)[None, :]
    owner = jnp.arange(remote_keys.shape[0], dtype=jnp.int32) // NB
    local = jnp.einsum("tkgd,skd->kgts", query, key_loc, preferred_element_type=jnp.float32) * scale
    local = jnp.where(causal[None, None], local, -jnp.inf)
    remote = (
        jnp.einsum("tkgd,skd->kgts", query, remote_keys, preferred_element_type=jnp.float32) * scale
    )
    remote = jnp.where((owner < index)[None, None, None, :], remote, -jnp.inf)
    scores = jnp.concatenate([local, remote], axis=-1)
    top = jnp.max(scores, axis=-1, keepdims=True)
    expo = jnp.exp(scores - top)
    weights = (expo / jnp.sum(expo, axis=-1, keepdims=True)).astype(jnp.bfloat16)
    every_value = jnp.concatenate(
        [values.reshape(tokens_here, KVH, HD), all_values.reshape(-1, KVH, HD)], axis=0
    )
    attended = jnp.einsum(
        "kgts,skd->tkgd", weights, every_value, preferred_element_type=jnp.float32
    )
    attended = attended.reshape(tokens_here, HQ * HD).astype(jnp.bfloat16)
    hidden = jnp.dot(
        attended,
        lax.all_gather(out_weight, "ctx", axis=0, tiled=True),
        preferred_element_type=jnp.float32,
    )
    normed = (normalize(hidden) * norm_gain).astype(jnp.bfloat16)
    flat_routes = routes.reshape(-1)
    hits = (flat_routes[:, None] == jnp.arange(experts_all, dtype=jnp.int32)[None, :]).astype(
        jnp.int32
    )
    slot = jnp.sum(hits * (jnp.cumsum(hits, axis=0) - 1), axis=-1)
    target = flat_routes * capacity + slot
    source = jnp.arange(tokens_here * TOP, dtype=jnp.int32) // TOP
    outgoing = jnp.zeros((experts_all * capacity, D), jnp.bfloat16).at[target].set(normed[source])
    outgoing = outgoing.reshape(experts_all, capacity, D)
    arrived = lax.all_to_all(outgoing, "ctx", split_axis=0, concat_axis=0, tiled=True)
    senders = arrived.shape[0] // EXP_DEV
    width = arrived.shape[1]
    inputs = (
        arrived.reshape(senders, EXP_DEV, width, D)
        .transpose(1, 0, 2, 3)
        .reshape(EXP_DEV, senders * width, D)
    )
    gate = jnp.einsum("erd,edf->erf", inputs, expert_gate, preferred_element_type=jnp.float32)
    upper = jnp.einsum("erd,edf->erf", inputs, expert_up, preferred_element_type=jnp.float32)
    act = (jax.nn.silu(gate) * upper).astype(jnp.bfloat16)
    result = jnp.einsum(
        "erf,efd->erd", act, expert_down, preferred_element_type=jnp.float32
    ).astype(jnp.bfloat16)
    result = (
        result.reshape(EXP_DEV, senders, width, D)
        .transpose(1, 0, 2, 3)
        .reshape(senders * EXP_DEV, width, D)
    )
    returned = lax.all_to_all(result, "ctx", split_axis=0, concat_axis=0, tiled=True)
    returned = returned.reshape(experts_all * capacity, D)
    picked = jnp.take(returned, target, axis=0).reshape(tokens_here, TOP, D)
    blended = jnp.sum(combine[:, :, None] * picked.astype(jnp.float32), axis=1)
    return (hidden.astype(jnp.bfloat16), (hidden + blended).astype(jnp.bfloat16))


def solution(mesh):
    in_specs = (
        P(("groups", "ctx"), None),
        P(("groups", "ctx"), None),
        P(("groups", "ctx"), None),
        P(("groups", "ctx")),
        P("ctx", None),
        P(),
        P(),
        P(("groups", "ctx"), None),
        P(("groups", "ctx"), None),
        P("ctx", None, None),
        P("ctx", None, None),
        P("ctx", None, None),
    )
    out_specs = (P(("groups", "ctx"), None), P(("groups", "ctx"), None))
    return jax.shard_map(body, mesh=mesh, in_specs=in_specs, out_specs=out_specs, check_vma=False)
```

profile of v0, /device:TPU:0, one launch (start us, length us, event | category | flops | bytes accessed | tf_op | source)
XLA Modules:
  0.0 147.0 jit_solution(8379476434412805162)
XLA Ops:
  0.6 144.0 %shard_map.131 = (bf16[128,2048]{1,0:T(8,128)(2,1)}, bf16[128,2048]{1,0:T(8,128)(2,1)}) custom-call(bf16[128,2048]{1,0:T(8,128)(2,1)} %queries.1, bf16[128,512]{1,0:T(8,128)(2,1)} %keys.1, bf16[128,512]{1,0:T(8,128)(2,1)} %values.1, s32[1,128]{1,0:T(1,128)} %bitcast.14, bf16[128,2048]{1,0:T(8,128)(2,1)} %weight_own.1, f32[1,128]{1,0:T(1,128)} %bitcast.15, ...), custom_call_target="tpu_custom_call" | custom-call | tf_op jit(solution)/shard_map/pallas_call | solution.py:589
  144.6 2.2 %shard_map.132 = (bf16[128,2048]{1,0:T(8,128)(2,1)}, bf16[128,2048]{1,0:T(8,128)(2,1)}) custom-call(bf16[128,2048]{1,0:T(8,128)(2,1)} %get-tuple-element.4.a, bf16[128,2048]{1,0:T(8,128)(2,1)} %get-tuple-element.5.b), custom_call_target="tpu_custom_call" | custom-call | tf_op jit(solution)/shard_map/pallas_call | solution.py:652
where the time goes:
time: 147 us
  Pallas kernels  146 us (99%)
    pallas_call x1, Pallas kernels, layer_ring(): pl.pallas_call(functools.partial(layer_kernel, n, cap), out_shape=(result...  144 us

commit v1 on v0

--- a/solution.py
+++ b/solution.py
@@ -22,6 +22,7 @@
 
 
 RING_BYTES = 16 * 2**20
+PASSES = 2
 
 
 def chip_at(position, chips):
@@ -50,7 +51,9 @@
     normed,
     hidden,
     att,
-    wg,
+    wq,
+    outq,
+    hidq,
     sums_own,
     sums,
     share,
@@ -72,10 +75,12 @@
     s_recv,
     wg_send,
     wg_recv,
-    wx_send,
-    wx_recv,
     wp_send,
     wp_recv,
+    at_send,
+    at_recv,
+    h_send,
+    h_recv,
     w_send,
     w_recv,
     ag_send,
@@ -119,6 +124,7 @@
 
     lax.fori_loop(1, n, greet, 0)
     pl.semaphore_signal(barrier, inc=1, device_id={"groups": across})
+    pl.semaphore_signal(barrier, inc=1, device_id={"groups": across, "ctx": partner})
 
     def mean_of(ref):
         shape = (2 * NB, tokens)
@@ -137,7 +143,7 @@
         sums_own[:, cols] = jnp.where(
             upper, normalize(kmean[:, cols]) * key_gain[...], normalize(vmean[:, cols])
         ).astype(jnp.bfloat16)
-    pl.semaphore_wait(barrier, n)
+    pl.semaphore_wait(barrier, n + 1)
 
     def s_copy(k):
         target = (me + k) % n
@@ -193,64 +199,81 @@
         return (0, 1) if d == 0 else (1, 0)
 
     wrows = weight_own.shape[0]
-    side = wrows // 4
-    middle = wrows - 2 * side
+    passes, pcols = wq.shape[0], wq.shape[3]
     group = 1 - across
-    mine_side = group * (side + middle)
-    other_side = across * (side + middle)
-
-    def w_rows(kind):
-        if kind == 0:
-            return mine_side, side
-        if kind == 1:
-            return side, middle
-        return other_side, side
-
-    def w_at(q, kind):
-        start, size = w_rows(kind)
-        return wg.at[q, pl.ds(core * wrows + start, size)]
-
-    def w_first(kind):
-        start, size = w_rows(kind)
-        return weight_own.at[pl.ds(start, size)]
-
-    def wg_copy(d, step, h):
+    slot = group * 2 + core
+
+    def own_rows(t):
+        return pl.ds(pl.multiple_of((core if t == 0 else 1 - core) * wrows, wrows), wrows)
+
+    def w_cols(t, p):
+        side = group * 2 + (core if t == 0 else 1 - core)
+        return pl.ds(pl.multiple_of((side * passes + p) * pcols, pcols), pcols)
+
+    def w_at(p, q, t):
+        return wq.at[p, chip_at(q, chips), own_rows(t)]
+
+    def wg_copy(d, step, p, t):
         sign = 1 - 2 * d
-        q = chip(-sign * (step - 1))
-        return pltpu.make_async_remote_copy(
-            src_ref=w_first(h) if step == 1 else w_at(q, h),
-            dst_ref=w_at(q, h),
-            send_sem=wg_send.at[d, step - 1, h],
-            recv_sem=wg_recv.at[d, step - 1, h],
-            device_id={"ctx": neighbour[d]},
-        )
-
-    def wx_copy(offset):
-        q = chip(offset)
-        return pltpu.make_async_remote_copy(
-            src_ref=w_at(q, 0),
-            dst_ref=w_at(q, 0),
-            send_sem=wx_send.at[offset % chips],
-            recv_sem=wx_recv.at[offset % chips],
-            device_id={"groups": across},
-        )
-
-    def wp_copy(offset, kind):
-        q = chip(offset)
-        return pltpu.make_async_remote_copy(
-            src_ref=w_first(kind) if offset == 0 else w_at(q, kind),
-            dst_ref=w_at(q, kind),
-            send_sem=wp_send.at[offset % chips, kind],
-            recv_sem=wp_recv.at[offset % chips, kind],
+        if step == 1:
+            src, dst = weight_own.at[:, w_cols(t, p)], w_at(p, pos, 0)
+            target = neighbour[d] + t * (1 - 2 * core)
+        else:
+            src = dst = w_at(p, chip(-sign * (step - 1)), t)
+            target = neighbour[d]
+        return pltpu.make_async_remote_copy(
+            src_ref=src,
+            dst_ref=dst,
+            send_sem=wg_send.at[d, step - 1, p, t],
+            recv_sem=wg_recv.at[d, step - 1, p, t],
+            device_id={"ctx": target},
+        )
+
+    def wp_copy(p):
+        return pltpu.make_async_remote_copy(
+            src_ref=weight_own.at[:, w_cols(1, p)],
+            dst_ref=w_at(p, pos, 0),
+            send_sem=wp_send.at[p],
+            recv_sem=wp_recv.at[p],
             device_id={"ctx": partner},
         )
 
-    for k in range(2):
-        for d in range(2):
-            wg_copy(d, 1, order(d)[k]).start()
-    for kind in range(3):
-        wp_copy(0, kind).start()
-    wg[pos, pl.ds(pl.multiple_of(core * wrows, wrows), wrows)] = weight_own[...]
+    def at_copy(kind, g):
+        span = HQ // KVH * HD
+        source = slot if kind < 2 else across * 2 + core
+        block = att.at[
+            pl.ds(pl.multiple_of(source * tokens, tokens), tokens), g * span : (g + 1) * span
+        ]
+        return pltpu.make_async_remote_copy(
+            src_ref=block,
+            dst_ref=block,
+            send_sem=at_send.at[kind, g],
+            recv_sem=at_recv.at[kind, g],
+            device_id={"groups": across} if kind == 1 else {"ctx": partner},
+        )
+
+    def h_copy(kind, p):
+        target = (
+            {"ctx": partner},
+            {"groups": across},
+            {"groups": across, "ctx": partner},
+        )[kind]
+        theirs_slot = (group, across, across)[kind] * 2 + (1 - core, core, 1 - core)[kind]
+        return pltpu.make_async_remote_copy(
+            src_ref=outq.at[p, theirs_slot],
+            dst_ref=hidq.at[slot, p],
+            send_sem=h_send.at[kind, p],
+            recv_sem=h_recv.at[kind, p],
+            device_id=target,
+        )
+
+    for p in range(passes):
+        for k in range(2):
+            for d in range(2):
+                wg_copy(d, 1, p, order(d)[k]).start()
+    for p in range(passes):
+        wp_copy(p).start()
+        wq[p, chip_at(pos, chips), own_rows(0)] = weight_own[:, w_cols(0, p)]
 
     def w_copy(k):
         target = (me + k) % n
@@ -318,64 +341,60 @@
         ) + jnp.dot(remote, shifted, preferred_element_type=jnp.float32)
         result = result.astype(jnp.bfloat16)
         for i, c in enumerate(heads):
-            att[:, c] = result[i * tokens : (i + 1) * tokens]
-
-    def project(offset):
-        q = chip(offset)
+            att[pl.ds(pl.multiple_of(slot * tokens, tokens), tokens), c] = result[
+                i * tokens : (i + 1) * tokens
+            ]
+        at_copy(1, g).start()
+        at_copy(0, g).start()
+
+    def project(p):
+        weight = wq[p].reshape(chips * 2 * wrows, pcols)
+        for side in (across, group):
+            left = att[pl.ds(pl.multiple_of(side * 2 * tokens, 2 * tokens), 2 * tokens)]
+            part = jnp.dot(left, weight, preferred_element_type=jnp.float32).astype(jnp.bfloat16)
+            for c in range(2):
+                outq[p, side * 2 + c] = part[c * tokens : (c + 1) * tokens]
+            if side is across:
+                h_copy(1, p).start()
+                h_copy(2, p).start()
+            else:
+                h_copy(0, p).start()
+        hidq[slot, p] = outq[p, slot]
+
+    def w_step(step, p):
+        for k in range(2):
+            for d in range(2):
+                t = order(d)[k]
+                if step < far or k == 0:
+                    wg_copy(d, step, p, t).wait_recv()
+                if step + 1 < far or (step + 1 == far and k == 0):
+                    wg_copy(d, step + 1, p, t).start()
+
+    for g in range(KVH):
+        attend(g)
+        if g > 0:
+            at_copy(1, g - 1).wait_recv()
+            at_copy(2, g - 1).start()
+        if g + 1 < far:
+            for p in range(passes):
+                w_step(g + 1, p)
+    at_copy(1, KVH - 1).wait_recv()
+    at_copy(2, KVH - 1).start()
+    for p in range(passes):
+        wp_copy(p).wait_recv()
+    for g in range(KVH):
+        at_copy(0, g).wait_recv()
+        at_copy(2, g).wait_recv()
+    for p in range(passes):
+        for step in range(min(KVH + 1, far), far + 1):
+            w_step(step, p)
+        project(p)
+    for p in range(passes):
         for kind in range(3):
-            wp_copy(offset, kind).wait_recv()
-        place_at = pl.multiple_of(chip_at(q, chips) * 2 * wrows, 2 * wrows)
-        left = att[:, pl.ds(place_at, 2 * wrows)]
-
-        def tile(k, _):
-            cols = pl.ds(pl.multiple_of(k * 512, 512), 512)
-            part = jnp.dot(left, wg[q, :, cols], preferred_element_type=jnp.float32)
-            hidden[:, cols] = part if offset == 0 else hidden[:, cols] + part
-            return 0
-
-        lax.fori_loop(0, width // 512, tile, 0)
-
-    def w_step(step, k):
-        for d in range(2):
-            h = order(d)[k]
-            sign = 1 - 2 * d
-            wg_copy(d, step, h).wait_recv()
-            if step + 1 < far or (step + 1 == far and k == 0):
-                wg_copy(d, step + 1, h).start()
-            if h == 0:
-                wx_copy(-sign * step).start()
-            wp_copy(-sign * step, h).start()
-
-    def x_step(offset):
-        wx_copy(offset).wait_recv()
-        wp_copy(offset, 2).start()
-
-    attend(0)
-    attend(1)
-    w_step(1, 0)
-    attend(2)
-    w_step(1, 1)
-    attend(3)
-    for step in range(2, far):
-        w_step(step, 0)
-        x_step(1 - step)
-        x_step(step - 1)
-        if step == 2:
-            project(0)
-        else:
-            project(2 - step)
-        w_step(step, 1)
-        if step > 2:
-            project(step - 2)
-    w_step(far, 0)
-    x_step(1 - far)
-    x_step(far - 1)
-    project(2 - far)
-    project(far - 2)
-    x_step(far)
-    project(1 - far)
-    project(far - 1)
-    project(far)
+            h_copy(kind, p).wait_recv()
+        for s in range(4):
+            at = (s * passes + p) * pcols
+            hidden[:, at : at + pcols] = hidq[s, p].astype(jnp.float32)
     for h in range(2):
         hid = hidden[rows(h)]
         projected[rows(h)] = hid.astype(jnp.bfloat16)
@@ -539,16 +558,18 @@
         y_copy(offset).wait_send()
 
 
-    for d in range(2):
-        for step in range(1, far + 1):
-            for k in range(2):
-                if step < far or k == 0:
-                    wg_copy(d, step, order(d)[k]).wait_send()
-    for offset in range(chips):
-        if offset > 0:
-            wx_copy(offset).wait_send()
+    for p in range(passes):
+        for d in range(2):
+            for step in range(1, far + 1):
+                for k in range(2):
+                    if step < far or k == 0:
+                        wg_copy(d, step, p, order(d)[k]).wait_send()
+        wp_copy(p).wait_send()
         for kind in range(3):
-            wp_copy(offset, kind).wait_send()
+            h_copy(kind, p).wait_send()
+    for g in range(KVH):
+        for kind in range(3):
+            at_copy(kind, g).wait_send()
 
 
 def write_kernel(a, b, a_out, b_out, sem):
@@ -594,8 +615,10 @@
         scratch_shapes=[
             pltpu.VMEM((tokens, width), bf16),
             pltpu.VMEM((tokens, width), f32),
-            pltpu.VMEM((tokens, width), bf16),
-            pltpu.VMEM((chips, 2 * out_weight.shape[0], width), bf16),
+            pltpu.VMEM((4 * tokens, width), bf16),
+            pltpu.VMEM((PASSES, chips, 2 * out_weight.shape[0], width // (4 * PASSES)), bf16),
+            pltpu.VMEM((PASSES, 4, tokens, width // (4 * PASSES)), bf16),
+            pltpu.VMEM((4, PASSES, tokens, width // (4 * PASSES)), bf16),
             pltpu.VMEM((2 * NB, KVH * HD), bf16),
             pltpu.VMEM((n, 2 * NB, KVH * HD), bf16),
             pltpu.VMEM((n, 8, tokens), f32),
@@ -615,12 +638,14 @@
             dma((3,)),
             dma((n,)),
             dma((n,)),
-            dma((2, far, 2)),
-            dma((2, far, 2)),
-            dma((chips,)),
-            dma((chips,)),
-            dma((chips, 3)),
-            dma((chips, 3)),
+            dma((2, far, PASSES, 2)),
+            dma((2, far, PASSES, 2)),
+            dma((PASSES,)),
+            dma((PASSES,)),
+            dma((3, KVH)),
+            dma((3, KVH)),
+            dma((3, PASSES)),
+            dma((3, PASSES)),
             dma((n,)),
             dma((n,)),
             dma((2, far, 2)),

time: 147 us -> 143 us (0.973)
  Pallas kernels: 146 us -> 142 us
    pallas_call x1, Pallas kernels: 144 us -> 140 us  [layer_ring(): pl.pallas_call(functools.partial(layer_kernel, n, cap), out_shape=(result...]
where the time goes in v1:
time: 143 us
  Pallas kernels  142 us (99%)
    pallas_call x1, Pallas kernels, layer_ring(): pl.pallas_call(functools.partial(layer_kernel, n, cap), out_shape=(result...  140 us

profile of v1, /device:TPU:0, one launch (start us, length us, event | category | flops | bytes accessed | tf_op | source)
XLA Modules:
  0.0 142.6 jit_solution(9068487172353048608)
XLA Ops:
  0.6 139.7 %shard_map.131 = (bf16[128,2048]{1,0:T(8,128)(2,1)}, bf16[128,2048]{1,0:T(8,128)(2,1)}) custom-call(bf16[128,2048]{1,0:T(8,128)(2,1)} %queries.1, bf16[128,512]{1,0:T(8,128)(2,1)} %keys.1, bf16[128,512]{1,0:T(8,128)(2,1)} %values.1, s32[1,128]{1,0:T(1,128)} %bitcast.14, bf16[128,2048]{1,0:T(8,128)(2,1)} %weight_own.1, f32[1,128]{1,0:T(1,128)} %bitcast.15, ...), custom_call_target="tpu_custom_call" | custom-call | tf_op jit(solution)/shard_map/pallas_call | solution.py:610
  140.3 2.2 %shard_map.132 = (bf16[128,2048]{1,0:T(8,128)(2,1)}, bf16[128,2048]{1,0:T(8,128)(2,1)}) custom-call(bf16[128,2048]{1,0:T(8,128)(2,1)} %get-tuple-element.4.a, bf16[128,2048]{1,0:T(8,128)(2,1)} %get-tuple-element.5.b), custom_call_target="tpu_custom_call" | custom-call | tf_op jit(solution)/shard_map/pallas_call | solution.py:677

commit v2 on v1

--- a/solution.py
+++ b/solution.py
@@ -23,6 +23,7 @@
 
 RING_BYTES = 16 * 2**20
 PASSES = 2
+OUT_TILE = 1024
 
 
 def chip_at(position, chips):
@@ -62,6 +63,7 @@
     down_w,
     tok,
     wbuf,
+    slots,
     rows_in,
     act,
     place,
@@ -146,24 +148,49 @@
     pl.semaphore_wait(barrier, n + 1)
 
     def s_copy(k):
-        target = (me + k) % n
         return pltpu.make_async_remote_copy(
             src_ref=sums_own,
             dst_ref=sums.at[me],
             send_sem=s_send.at[k],
             recv_sem=s_recv.at[k],
-            device_id={"ctx": target},
-        )
+            device_id={"ctx": (me + 2 * k) % n},
+        )
+
+    def sp_copy(k):
+        source = (me + n - 2 * k) % n
+        return pltpu.make_async_remote_copy(
+            src_ref=sums.at[source],
+            dst_ref=sums.at[source],
+            send_sem=s_send.at[chips + k],
+            recv_sem=s_recv.at[chips + k],
+            device_id={"ctx": partner},
+        )
+
+    own_copy = pltpu.make_async_remote_copy(
+        src_ref=sums_own,
+        dst_ref=sums.at[me],
+        send_sem=s_send.at[chips],
+        recv_sem=s_recv.at[chips],
+        device_id={"ctx": partner},
+    )
 
     def s_start(k, _):
         s_copy(k).start()
         return 0
 
+    def s_pass(k, _):
+        s_copy(k).wait_recv()
+        sp_copy(k).start()
+        return 0
+
     def s_wait(k, _):
-        s_copy(k).wait()
+        sp_copy(k).wait_recv()
+        s_copy(k).wait_send()
+        sp_copy(k).wait_send()
         return 0
 
-    lax.fori_loop(1, n, s_start, 0)
+    lax.fori_loop(1, chips, s_start, 0)
+    own_copy.start()
     sums[me] = sums_own[...]
 
     def rows(h):
@@ -300,10 +327,12 @@
     for c in range(TOP):
         table_of = table_of + jnp.where(routes[c : c + 1] == expert, combine[c : c + 1], 0.0)
     for e in range(n):
-        share[e] = jnp.broadcast_to(table_of[e : e + 1], (8, tokens))
+        share[e] = table_of[e : e + 1]
     lax.fori_loop(1, n, w_start, 0)
     wbuf[pos * 2 + core] = share[me]
-    lax.fori_loop(1, n, s_wait, 0)
+    lax.fori_loop(1, chips, s_pass, 0)
+    own_copy.wait()
+    lax.fori_loop(1, chips, s_wait, 0)
 
     many = HQ // KVH
     scale = 1.0 / math.sqrt(HD)
@@ -408,9 +437,20 @@
     for h in range(2):
         pt_copy(0, h).start()
 
-    lax.fori_loop(1, n, w_wait, 0)
-    for load in loads:
-        load.wait()
+    def prepare():
+        lax.fori_loop(1, n, w_wait, 0)
+        weight = wbuf[...].reshape(n, tokens)
+        earlier = lax.broadcasted_iota(jnp.int32, (tokens, tokens), 0) < lax.broadcasted_iota(
+            jnp.int32, (tokens, tokens), 1
+        )
+        earlier = jnp.where(earlier, 1.0, 0.0).astype(jnp.bfloat16)
+        chosen = jnp.where(weight > 0.0, 1.0, 0.0).astype(jnp.bfloat16)
+        slot_of = jnp.dot(chosen, earlier, preferred_element_type=jnp.float32)
+        slot_of = jnp.where(weight > 0.0, slot_of, -1.0)
+        for e in range(n):
+            slots[e] = slot_of[e : e + 1]
+        for load in loads:
+            load.wait()
 
     def y_copy(offset):
         q = chip(offset)
@@ -422,78 +462,81 @@
             device_id={"ctx": partner},
         )
 
-    def compute(offset):
-        q = chip(offset)
-        for h in range(2):
-            pt_copy(offset, h).wait_recv()
-        earlier = lax.broadcasted_iota(jnp.int32, (tokens, tokens), 0) < lax.broadcasted_iota(
-            jnp.int32, (tokens, tokens), 1
-        )
-        earlier = jnp.where(earlier, 1.0, 0.0).astype(jnp.bfloat16)
+    def gather(offsets):
         line = lax.broadcasted_iota(jnp.int32, (cap, tokens), 0).astype(jnp.float32)
-        for rel in range(2):
-            side = (core + rel) % 2
-            weight = wbuf[q * 2 + side]
-            chosen = jnp.where(weight > 0.0, 1.0, 0.0)
-            slot = jnp.dot(chosen.astype(jnp.bfloat16), earlier, preferred_element_type=jnp.float32)
-            slot = jnp.where(weight > 0.0, slot, -1.0)
-            hit = jnp.broadcast_to(slot[0:1], (cap, tokens)) == line
-            pick = jnp.where(hit, 1.0, 0.0).astype(jnp.bfloat16)
-            place[rel] = pick
-            scaled = jnp.where(hit, jnp.broadcast_to(weight[0:1], (cap, tokens)), 0.0)
-            comb[rel] = jnp.broadcast_to(jnp.sum(scaled, axis=1, keepdims=True), (cap, 128))
-            for c in range(0, width, 512):
-                rows_in[rel * cap : (rel + 1) * cap, c : c + 512] = jnp.dot(
-                    pick, tok[q, side, :, c : c + 512], preferred_element_type=jnp.float32
-                ).astype(jnp.bfloat16)
+        for i, offset in enumerate(offsets):
+            q = chip(offset)
+            for h in range(2):
+                pt_copy(offset, h).wait_recv()
+            for rel in range(2):
+                side = (core + rel) % 2
+                j = 2 * i + rel
+                hit = jnp.broadcast_to(slots[q * 2 + side], (cap, tokens)) == line
+                pick = jnp.where(hit, 1.0, 0.0).astype(jnp.bfloat16)
+                place[j] = pick
+                scaled = jnp.where(hit, jnp.broadcast_to(wbuf[q * 2 + side], (cap, tokens)), 0.0)
+                comb[j] = jnp.broadcast_to(jnp.sum(scaled, axis=1, keepdims=True), (cap, 128))
+                for c in range(0, width, 512):
+                    rows_in[j * cap : (j + 1) * cap, c : c + 512] = jnp.dot(
+                        pick, tok[q, side, :, c : c + 512], preferred_element_type=jnp.float32
+                    ).astype(jnp.bfloat16)
+
+    def expand(offsets):
+        many_rows = len(offsets) * 2 * cap
 
         def in_tile(k, _):
             cols = pl.ds(pl.multiple_of(k * 256, 256), 256)
-            x = rows_in[...]
+            x = rows_in[:many_rows]
             g = jnp.dot(x, gate_w[:, cols], preferred_element_type=jnp.float32)
             u = jnp.dot(x, up_w[:, cols], preferred_element_type=jnp.float32)
-            act[:, cols] = (g / (1.0 + jnp.exp(-g)) * u).astype(jnp.bfloat16)
+            act[:many_rows, cols] = (g / (1.0 + jnp.exp(-g)) * u).astype(jnp.bfloat16)
             return 0
 
         lax.fori_loop(0, ff // 256, in_tile, 0)
 
+    def finish(offsets):
+        many_rows = len(offsets) * 2 * cap
+
         def out_tile(k, _):
-            cols = pl.ds(pl.multiple_of(k * 512, 512), 512)
-            r = jnp.dot(act[...], down_w[:, cols], preferred_element_type=jnp.float32)
+            cols = pl.ds(pl.multiple_of(k * OUT_TILE, OUT_TILE), OUT_TILE)
+            r = jnp.dot(act[:many_rows], down_w[:, cols], preferred_element_type=jnp.float32)
             r = r.astype(jnp.bfloat16).astype(jnp.float32)
-            for rel, dest in ((0, mine), (1, outgo)):
-                part = r[rel * cap : (rel + 1) * cap] * comb[rel][:, 0:1]
-                dest[q, :, cols] = lax.dot_general(
-                    place[rel],
-                    part.astype(jnp.bfloat16),
-                    (((0,), (0,)), ((), ())),
-                    preferred_element_type=jnp.float32,
-                ).astype(jnp.bfloat16)
+            for i, offset in enumerate(offsets):
+                for rel, dest in ((0, mine), (1, outgo)):
+                    j = 2 * i + rel
+                    part = r[j * cap : (j + 1) * cap] * comb[j][:, 0:1]
+                    dest[chip(offset), :, cols] = lax.dot_general(
+                        place[j],
+                        part.astype(jnp.bfloat16),
+                        (((0,), (0,)), ((), ())),
+                        preferred_element_type=jnp.float32,
+                    ).astype(jnp.bfloat16)
             return 0
 
-        lax.fori_loop(0, width // 512, out_tile, 0)
-        y_copy(offset).start()
-
+        lax.fori_loop(0, width // OUT_TILE, out_tile, 0)
+        for offset in offsets:
+            y_copy(offset).start()
+
+    def relay(step, k):
+        for d in range(2):
+            h = order(d)[k]
+            sign = 1 - 2 * d
+            ag_copy(d, step, h).wait_recv()
+            if step + 1 < far or (step + 1 == far and k == 0):
+                ag_copy(d, step + 1, h).start()
+            pt_copy(-sign * step, h).start()
+
+    relay(1, 0)
+    prepare()
+    relay(1, 1)
     for step in range(1, far):
-        for k in range(2):
-            for d in range(2):
-                h = order(d)[k]
-                sign = 1 - 2 * d
-                ag_copy(d, step, h).wait_recv()
-                if step + 1 < far or k == 0:
-                    ag_copy(d, step + 1, h).start()
-                pt_copy(-sign * step, h).start()
-            if step == 1:
-                if k == 0:
-                    compute(0)
-            else:
-                compute((step - 1) * (2 * k - 1))
-    compute(1 - far)
-    compute(far - 1)
-    for d in range(2):
-        h = order(d)[0]
-        ag_copy(d, far, h).wait_recv()
-        pt_copy(far, h).start()
+        pair = (-step, step)
+        gather(pair)
+        expand(pair)
+        relay(step + 1, 0)
+        finish(pair)
+        if step + 1 < far:
+            relay(step + 1, 1)
 
     def sum_of(q, h):
         return mine[q, rows(h)].astype(jnp.float32) + theirs[q, rows(h)].astype(jnp.float32)
@@ -522,21 +565,29 @@
             ).astype(jnp.bfloat16)
         rs_copy(d, step, h, src).start()
 
-    for offset in range(chips):
-        if offset != far:
+    gather((far,))
+    for step in range(1, far):
+        for offset in (-step, step):
             y_copy(offset).wait_recv()
     for d in range(2):
         rs_step(d, 2, 1)
-    compute(far)
-    y_copy(far).wait_recv()
+    expand((far,))
+    finish((far,))
     sends = [(1, 0)]
     for step in range(2, far + 1):
         if step < far:
             sends += [(step + 1, 1)]
         sends += [(step, 0)]
-    for step, k in sends:
+    y_copy(far).wait_recv()
+    for i, (step, k) in enumerate(sends):
         for d in range(2):
             rs_step(d, step, k)
+        if i == 1:
+            gather((0,))
+            expand((0,))
+        if i == 2:
+            finish((0,))
+    y_copy(0).wait_recv()
     for h in range(2):
         total = hidden[rows(h)] + sum_of(pos, h)
         for d in range(2):
@@ -621,16 +672,17 @@
             pltpu.VMEM((4, PASSES, tokens, width // (4 * PASSES)), bf16),
             pltpu.VMEM((2 * NB, KVH * HD), bf16),
             pltpu.VMEM((n, 2 * NB, KVH * HD), bf16),
-            pltpu.VMEM((n, 8, tokens), f32),
+            pltpu.VMEM((n, 1, tokens), f32),
             pltpu.VMEM((width, ff), bf16),
             pltpu.VMEM((width, ff), bf16),
             pltpu.VMEM((ff, width), bf16),
             pltpu.VMEM((chips, 2, tokens, width), bf16),
-            pltpu.VMEM((n, 8, tokens), f32),
-            pltpu.VMEM((2 * cap, width), bf16),
-            pltpu.VMEM((2 * cap, ff), bf16),
-            pltpu.VMEM((2, cap, tokens), bf16),
-            pltpu.VMEM((2, cap, 128), f32),
+            pltpu.VMEM((n, 1, tokens), f32),
+            pltpu.VMEM((n, 1, tokens), f32),
+            pltpu.VMEM((4 * cap, width), bf16),
+            pltpu.VMEM((4 * cap, ff), bf16),
+            pltpu.VMEM((4, cap, tokens), bf16),
+            pltpu.VMEM((4, cap, 128), f32),
             pltpu.VMEM((chips, tokens, width), bf16),
             pltpu.VMEM((chips, tokens, width), bf16),
             pltpu.VMEM((chips, tokens, width), bf16),

time: 143 us -> 137 us (0.958)
  Pallas kernels: 142 us -> 136 us
    pallas_call x1, Pallas kernels: 140 us -> 134 us  [layer_ring(): pl.pallas_call(functools.partial(layer_kernel, n, cap), out_shape=(result...]
where the time goes in v2:
time: 137 us
  Pallas kernels  136 us (99%)
    pallas_call x1, Pallas kernels, layer_ring(): pl.pallas_call(functools.partial(layer_kernel, n, cap), out_shape=(result...  134 us

profile of v2, /device:TPU:0, one launch (start us, length us, event | category | flops | bytes accessed | tf_op | source)
XLA Modules:
  0.0 137.0 jit_solution(11054566333963220919)
XLA Ops:
  0.6 134.0 %shard_map.131 = (bf16[128,2048]{1,0:T(8,128)(2,1)}, bf16[128,2048]{1,0:T(8,128)(2,1)}) custom-call(bf16[128,2048]{1,0:T(8,128)(2,1)} %queries.1, bf16[128,512]{1,0:T(8,128)(2,1)} %keys.1, bf16[128,512]{1,0:T(8,128)(2,1)} %values.1, s32[1,128]{1,0:T(1,128)} %bitcast.14, bf16[128,2048]{1,0:T(8,128)(2,1)} %weight_own.1, f32[1,128]{1,0:T(1,128)} %bitcast.15, ...), custom_call_target="tpu_custom_call" | custom-call | tf_op jit(solution)/shard_map/pallas_call | solution.py:661
  134.6 2.2 %shard_map.132 = (bf16[128,2048]{1,0:T(8,128)(2,1)}, bf16[128,2048]{1,0:T(8,128)(2,1)}) custom-call(bf16[128,2048]{1,0:T(8,128)(2,1)} %get-tuple-element.4.a, bf16[128,2048]{1,0:T(8,128)(2,1)} %get-tuple-element.5.b), custom_call_target="tpu_custom_call" | custom-call | tf_op jit(solution)/shard_map/pallas_call | solution.py:729

commit v3 on v2

--- a/solution.py
+++ b/solution.py
@@ -23,7 +23,7 @@
 
 RING_BYTES = 16 * 2**20
 PASSES = 2
-OUT_TILE = 1024
+PARTS = 2
 
 
 def chip_at(position, chips):
@@ -68,8 +68,7 @@
     act,
     place,
     comb,
-    mine,
-    outgo,
+    results,
     theirs,
     ring_in,
     load_sem,
@@ -449,16 +448,22 @@
         slot_of = jnp.where(weight > 0.0, slot_of, -1.0)
         for e in range(n):
             slots[e] = slot_of[e : e + 1]
+        place[...] = jnp.zeros_like(place)
         for load in loads:
             load.wait()
 
-    def y_copy(offset):
+    part_width = width // PARTS
+
+    def cols_of(c):
+        return slice(c * part_width, (c + 1) * part_width)
+
+    def y_copy(offset, c):
         q = chip(offset)
         return pltpu.make_async_remote_copy(
-            src_ref=outgo.at[q],
-            dst_ref=theirs.at[q],
-            send_sem=y_send.at[offset % chips],
-            recv_sem=y_recv.at[offset % chips],
+            src_ref=results.at[q, 1 - core, :, cols_of(c)],
+            dst_ref=theirs.at[q, :, cols_of(c)],
+            send_sem=y_send.at[offset % chips, c],
+            recv_sem=y_recv.at[offset % chips, c],
             device_id={"ctx": partner},
         )
 
@@ -466,20 +471,25 @@
         line = lax.broadcasted_iota(jnp.int32, (cap, tokens), 0).astype(jnp.float32)
         for i, offset in enumerate(offsets):
             q = chip(offset)
+            for side in range(2):
+                hit = jnp.broadcast_to(slots[q * 2 + side], (cap, tokens)) == line
+                pick = jnp.where(hit, 1.0, 0.0).astype(jnp.bfloat16)
+                span = slice(side * cap, (side + 1) * cap)
+                place[i, span, side * tokens : (side + 1) * tokens] = pick
+                scaled = jnp.where(hit, jnp.broadcast_to(wbuf[q * 2 + side], (cap, tokens)), 0.0)
+                comb[i, span] = jnp.broadcast_to(
+                    jnp.sum(scaled, axis=1, keepdims=True), (cap, 128)
+                )
+        for i, offset in enumerate(offsets):
+            q = chip(offset)
             for h in range(2):
                 pt_copy(offset, h).wait_recv()
-            for rel in range(2):
-                side = (core + rel) % 2
-                j = 2 * i + rel
-                hit = jnp.broadcast_to(slots[q * 2 + side], (cap, tokens)) == line
-                pick = jnp.where(hit, 1.0, 0.0).astype(jnp.bfloat16)
-                place[j] = pick
-                scaled = jnp.where(hit, jnp.broadcast_to(wbuf[q * 2 + side], (cap, tokens)), 0.0)
-                comb[j] = jnp.broadcast_to(jnp.sum(scaled, axis=1, keepdims=True), (cap, 128))
-                for c in range(0, width, 512):
-                    rows_in[j * cap : (j + 1) * cap, c : c + 512] = jnp.dot(
-                        pick, tok[q, side, :, c : c + 512], preferred_element_type=jnp.float32
-                    ).astype(jnp.bfloat16)
+            for c in range(0, width, 512):
+                rows_in[i * 2 * cap : (i + 1) * 2 * cap, c : c + 512] = jnp.dot(
+                    place[i],
+                    tok[q, :, :, c : c + 512].reshape(2 * tokens, 512),
+                    preferred_element_type=jnp.float32,
+                ).astype(jnp.bfloat16)
 
     def expand(offsets):
         many_rows = len(offsets) * 2 * cap
@@ -496,26 +506,25 @@
 
     def finish(offsets):
         many_rows = len(offsets) * 2 * cap
-
-        def out_tile(k, _):
-            cols = pl.ds(pl.multiple_of(k * OUT_TILE, OUT_TILE), OUT_TILE)
-            r = jnp.dot(act[:many_rows], down_w[:, cols], preferred_element_type=jnp.float32)
+        for c in range(PARTS):
+            r = jnp.dot(
+                act[:many_rows], down_w[:, cols_of(c)], preferred_element_type=jnp.float32
+            )
             r = r.astype(jnp.bfloat16).astype(jnp.float32)
             for i, offset in enumerate(offsets):
-                for rel, dest in ((0, mine), (1, outgo)):
-                    j = 2 * i + rel
-                    part = r[j * cap : (j + 1) * cap] * comb[j][:, 0:1]
-                    dest[chip(offset), :, cols] = lax.dot_general(
-                        place[j],
-                        part.astype(jnp.bfloat16),
-                        (((0,), (0,)), ((), ())),
-                        preferred_element_type=jnp.float32,
-                    ).astype(jnp.bfloat16)
-            return 0
-
-        lax.fori_loop(0, width // OUT_TILE, out_tile, 0)
-        for offset in offsets:
-            y_copy(offset).start()
+                part = r[i * 2 * cap : (i + 1) * 2 * cap] * comb[i][:, 0:1]
+                spread = lax.dot_general(
+                    place[i],
+                    part.astype(jnp.bfloat16),
+                    (((0,), (0,)), ((), ())),
+                    preferred_element_type=jnp.float32,
+                ).astype(jnp.bfloat16)
+                for side in range(2):
+                    results[chip(offset), side, :, cols_of(c)] = spread[
+                        side * tokens : (side + 1) * tokens
+                    ]
+            for offset in offsets:
+                y_copy(offset, c).start()
 
     def relay(step, k):
         for d in range(2):
@@ -533,67 +542,82 @@
         pair = (-step, step)
         gather(pair)
         expand(pair)
-        relay(step + 1, 0)
+        if step + 1 < far:
+            relay(step + 1, 0)
         finish(pair)
         if step + 1 < far:
             relay(step + 1, 1)
 
-    def sum_of(q, h):
-        return mine[q, rows(h)].astype(jnp.float32) + theirs[q, rows(h)].astype(jnp.float32)
-
-    def rs_copy(d, step, h, src):
+    def sum_of(q, h, c):
+        own = results[q, core, rows(h), cols_of(c)].astype(jnp.float32)
+        return own + theirs[q, rows(h), cols_of(c)].astype(jnp.float32)
+
+    def rs_copy(d, step, h, c, src):
         return pltpu.make_async_remote_copy(
             src_ref=src,
-            dst_ref=ring_in.at[d, step - 1, h],
-            send_sem=rs_send_sem.at[d, step - 1, h],
-            recv_sem=rs_recv_sem.at[d, step - 1, h],
+            dst_ref=ring_in.at[d, step - 1, h, :, cols_of(c)],
+            send_sem=rs_send_sem.at[d, step - 1, h, c],
+            recv_sem=rs_recv_sem.at[d, step - 1, h, c],
             device_id={"ctx": neighbour[d]},
         )
 
-    def rs_step(d, step, k):
+    def landed(d, step, h, c):
+        return ring_in.at[d, step - 1, h, :, cols_of(c)]
+
+    def rs_part(d, step, k, c):
         h = order(d)[k]
         sign = 1 - 2 * d
         q = chip(sign * (far + 1 - step))
         if step == 1 or (step == 2 and k == 1):
-            mine[q, rows(h)] = sum_of(q, h).astype(jnp.bfloat16)
-            src = mine.at[q, rows(h)]
+            results[q, core, rows(h), cols_of(c)] = sum_of(q, h, c).astype(jnp.bfloat16)
+            src = results.at[q, core, rows(h), cols_of(c)]
         else:
-            src = ring_in.at[d, step - 2, h]
-            rs_copy(d, step - 1, h, src).wait_recv()
-            ring_in[d, step - 2, h] = (
-                ring_in[d, step - 2, h].astype(jnp.float32) + sum_of(q, h)
+            src = landed(d, step - 1, h, c)
+            rs_copy(d, step - 1, h, c, src).wait_recv()
+            ring_in[d, step - 2, h, :, cols_of(c)] = (
+                ring_in[d, step - 2, h, :, cols_of(c)].astype(jnp.float32) + sum_of(q, h, c)
             ).astype(jnp.bfloat16)
-        rs_copy(d, step, h, src).start()
-
+        rs_copy(d, step, h, c, src).start()
+
+    def rs_step(step, k):
+        for c in range(PARTS):
+            for d in range(2):
+                rs_part(d, step, k, c)
+
+    for step in range(1, far - 1):
+        for offset in (-step, step):
+            for c in range(PARTS):
+                y_copy(offset, c).wait_recv()
+    for c in range(PARTS):
+        for d in range(2):
+            y_copy((1 - 2 * d) * (far - 1), c).wait_recv()
+            rs_part(d, 2, 1, c)
+    relay(far, 0)
     gather((far,))
-    for step in range(1, far):
-        for offset in (-step, step):
-            y_copy(offset).wait_recv()
-    for d in range(2):
-        rs_step(d, 2, 1)
     expand((far,))
     finish((far,))
-    sends = [(1, 0)]
+    for c in range(PARTS):
+        y_copy(far, c).wait_recv()
+        for d in range(2):
+            rs_part(d, 1, 0, c)
     for step in range(2, far + 1):
         if step < far:
-            sends += [(step + 1, 1)]
-        sends += [(step, 0)]
-    y_copy(far).wait_recv()
-    for i, (step, k) in enumerate(sends):
-        for d in range(2):
-            rs_step(d, step, k)
-        if i == 1:
+            rs_step(step + 1, 1)
+        if step == 2:
             gather((0,))
             expand((0,))
-        if i == 2:
+        rs_step(step, 0)
+        if step == 2:
             finish((0,))
-    y_copy(0).wait_recv()
-    for h in range(2):
-        total = hidden[rows(h)] + sum_of(pos, h)
-        for d in range(2):
-            rs_copy(d, far, h, ring_in.at[d, far - 1, h]).wait_recv()
-            total = total + ring_in[d, far - 1, h].astype(jnp.float32)
-        out[rows(h)] = total.astype(jnp.bfloat16)
+    for c in range(PARTS):
+        y_copy(0, c).wait_recv()
+    for c in range(PARTS):
+        for h in range(2):
+            total = hidden[rows(h), cols_of(c)] + sum_of(pos, h, c)
+            for d in range(2):
+                rs_copy(d, far, h, c, landed(d, far, h, c)).wait_recv()
+                total = total + ring_in[d, far - 1, h, :, cols_of(c)].astype(jnp.float32)
+            out[rows(h), cols_of(c)] = total.astype(jnp.bfloat16)
 
     for d in range(2):
         for step in range(1, far + 1):
@@ -602,11 +626,13 @@
                 if step < far or k == 0:
                     ag_copy(d, step, h).wait_send()
                 if step > 1 or k == 0:
-                    rs_copy(d, step, h, ring_in.at[d, step - 1, h]).wait_send()
+                    for c in range(PARTS):
+                        rs_copy(d, step, h, c, landed(d, step, h, c)).wait_send()
     for offset in range(chips):
         for h in range(2):
             pt_copy(offset, h).wait_send()
-        y_copy(offset).wait_send()
+        for c in range(PARTS):
+            y_copy(offset, c).wait_send()
 
 
     for p in range(passes):
@@ -681,10 +707,9 @@
             pltpu.VMEM((n, 1, tokens), f32),
             pltpu.VMEM((4 * cap, width), bf16),
             pltpu.VMEM((4 * cap, ff), bf16),
-            pltpu.VMEM((4, cap, tokens), bf16),
-            pltpu.VMEM((4, cap, 128), f32),
-            pltpu.VMEM((chips, tokens, width), bf16),
-            pltpu.VMEM((chips, tokens, width), bf16),
+            pltpu.VMEM((2, 2 * cap, 2 * tokens), bf16),
+            pltpu.VMEM((2, 2 * cap, 128), f32),
+            pltpu.VMEM((chips, 2, tokens, width), bf16),
             pltpu.VMEM((chips, tokens, width), bf16),
             pltpu.VMEM((2, far, 2, tokens // 2, width), bf16),
             dma((3,)),
@@ -704,10 +729,10 @@
             dma((2, far, 2)),
             dma((chips, 2)),
             dma((chips, 2)),
-            dma((chips,)),
-            dma((chips,)),
-            dma((2, far, 2)),
-            dma((2, far, 2)),
+            dma((chips, PARTS)),
+            dma((chips, PARTS)),
+            dma((2, far, 2, PARTS)),
+            dma((2, far, 2, PARTS)),
         ],
         compiler_params=pltpu.CompilerParams(
             collective_id=1, has_side_effects=True, vmem_limit_bytes=62 * 2**20

time: 137 us -> 134 us (0.978)
  Pallas kernels: 136 us -> 133 us
    pallas_call x1, Pallas kernels: 134 us -> 131 us  [layer_ring(): pl.pallas_call(functools.partial(layer_kernel, n, cap), out_shape=(result...]
where the time goes in v3:
time: 134 us
  Pallas kernels  133 us (99%)
    pallas_call x1, Pallas kernels, layer_ring(): pl.pallas_call(functools.partial(layer_kernel, n, cap), out_shape=(result...  131 us

profile of v3, /device:TPU:0, one launch (start us, length us, event | category | flops | bytes accessed | tf_op | source)
XLA Modules:
  0.0 134.1 jit_solution(17124633162047626169)
XLA Ops:
  0.6 131.1 %shard_map.131 = (bf16[128,2048]{1,0:T(8,128)(2,1)}, bf16[128,2048]{1,0:T(8,128)(2,1)}) custom-call(bf16[128,2048]{1,0:T(8,128)(2,1)} %queries.1, bf16[128,512]{1,0:T(8,128)(2,1)} %keys.1, bf16[128,512]{1,0:T(8,128)(2,1)} %values.1, s32[1,128]{1,0:T(1,128)} %bitcast.14, bf16[128,2048]{1,0:T(8,128)(2,1)} %weight_own.1, f32[1,128]{1,0:T(1,128)} %bitcast.15, ...), custom_call_target="tpu_custom_call" | custom-call | tf_op jit(solution)/shard_map/pallas_call | solution.py:687
  131.8 2.2 %shard_map.132 = (bf16[128,2048]{1,0:T(8,128)(2,1)}, bf16[128,2048]{1,0:T(8,128)(2,1)}) custom-call(bf16[128,2048]{1,0:T(8,128)(2,1)} %get-tuple-element.4.a, bf16[128,2048]{1,0:T(8,128)(2,1)} %get-tuple-element.5.b), custom_call_target="tpu_custom_call" | custom-call | tf_op jit(solution)/shard_map/pallas_call | solution.py:754

commit v4 on v3

--- a/solution.py
+++ b/solution.py
@@ -398,43 +398,50 @@
                 if step + 1 < far or (step + 1 == far and k == 0):
                     wg_copy(d, step + 1, p, t).start()
 
+    def hand_on(g):
+        at_copy(1, g).wait_recv()
+        at_copy(2, g).start()
+
+    hops = [(step, p) for step in range(1, far) for p in range(passes)]
+    w_step(*hops.pop(0))
     for g in range(KVH):
         attend(g)
-        if g > 0:
-            at_copy(1, g - 1).wait_recv()
-            at_copy(2, g - 1).start()
-        if g + 1 < far:
-            for p in range(passes):
-                w_step(g + 1, p)
-    at_copy(1, KVH - 1).wait_recv()
-    at_copy(2, KVH - 1).start()
+        if g > 1:
+            hand_on(g - 2)
+        if g + 1 < KVH:
+            w_step(*hops.pop(0))
+    for hop in hops:
+        w_step(*hop)
+    for g in range(KVH - 2, KVH):
+        hand_on(g)
     for p in range(passes):
         wp_copy(p).wait_recv()
     for g in range(KVH):
         at_copy(0, g).wait_recv()
         at_copy(2, g).wait_recv()
     for p in range(passes):
-        for step in range(min(KVH + 1, far), far + 1):
-            w_step(step, p)
+        w_step(far, p)
         project(p)
+    square = jnp.zeros((tokens, 1), jnp.float32)
     for p in range(passes):
         for kind in range(3):
             h_copy(kind, p).wait_recv()
         for s in range(4):
             at = (s * passes + p) * pcols
-            hidden[:, at : at + pcols] = hidq[s, p].astype(jnp.float32)
+            block = hidq[s, p].astype(jnp.float32)
+            hidden[:, at : at + pcols] = block
+            square = square + jnp.sum(block * block, axis=1, keepdims=True)
+    inverse = lax.rsqrt(square / width + 1e-06)
     for h in range(2):
-        hid = hidden[rows(h)]
-        projected[rows(h)] = hid.astype(jnp.bfloat16)
-        tidy = (normalize(hid) * norm_gain[...]).astype(jnp.bfloat16)
-        normed[rows(h)] = tidy
-        tok[pos, core, rows(h)] = tidy
-
-    for k in range(2):
-        for d in range(2):
-            ag_copy(d, 1, order(d)[k]).start()
+        tidy = hidden[rows(h)] * inverse[h * half : (h + 1) * half] * norm_gain[...]
+        normed[rows(h)] = tidy.astype(jnp.bfloat16)
+        ag_copy(h, 1, h).start()
+    for d in range(2):
+        ag_copy(d, 1, 1 - d).start()
     for h in range(2):
         pt_copy(0, h).start()
+    projected[...] = hidden[...].astype(jnp.bfloat16)
+    tok[pos, core] = normed[...]
 
     def prepare():
         lax.fori_loop(1, n, w_wait, 0)

time: 134 us -> 130 us (0.970)
  Pallas kernels: 133 us -> 129 us
    pallas_call x1, Pallas kernels: 131 us -> 127 us  [layer_ring(): pl.pallas_call(functools.partial(layer_kernel, n, cap), out_shape=(result...]
where the time goes in v4:
time: 130 us
  Pallas kernels  129 us (99%)
    pallas_call x1, Pallas kernels, layer_ring(): pl.pallas_call(functools.partial(layer_kernel, n, cap), out_shape=(result...  127 us

profile of v4, /device:TPU:0, one launch (start us, length us, event | category | flops | bytes accessed | tf_op | source)
XLA Modules:
  0.0 130.1 jit_solution(12847292573092508824)
XLA Ops:
  0.6 127.1 %shard_map.131 = (bf16[128,2048]{1,0:T(8,128)(2,1)}, bf16[128,2048]{1,0:T(8,128)(2,1)}) custom-call(bf16[128,2048]{1,0:T(8,128)(2,1)} %queries.1, bf16[128,512]{1,0:T(8,128)(2,1)} %keys.1, bf16[128,512]{1,0:T(8,128)(2,1)} %values.1, s32[1,128]{1,0:T(1,128)} %bitcast.14, bf16[128,2048]{1,0:T(8,128)(2,1)} %weight_own.1, f32[1,128]{1,0:T(1,128)} %bitcast.15, ...), custom_call_target="tpu_custom_call" | custom-call | tf_op jit(solution)/shard_map/pallas_call | solution.py:694
  127.8 2.2 %shard_map.132 = (bf16[128,2048]{1,0:T(8,128)(2,1)}, bf16[128,2048]{1,0:T(8,128)(2,1)}) custom-call(bf16[128,2048]{1,0:T(8,128)(2,1)} %get-tuple-element.4.a, bf16[128,2048]{1,0:T(8,128)(2,1)} %get-tuple-element.5.b), custom_call_target="tpu_custom_call" | custom-call | tf_op jit(solution)/shard_map/pallas_call | solution.py:761
